TPU v7x, 256 devices: a whole 4x4x8 slice. The times are simulated.
256 devices in a mesh: section: 2 (over y_lo), dp: 16 (over z, y_hi), tensor: 8 (over x, core).
Axes of the slice: x: 4, y: 4 (y_hi: 2, y_lo: 2; y = y_hi * 2 + y_lo), z: 8, core: 2. Of those that a mesh axis runs over, the one named last changes fastest.
Arguments:
- fwd_in: bfloat16 [2, 1024, 8192], P('section', 'tensor', 'dp'), may hold values from -6 to 6
- grad_in: bfloat16 [2, 1024, 8192], P('section', 'tensor', 'dp'), may hold values from -6 to 6
- saved_gate: bfloat16 [2, 1024, 14336], P('section', 'dp', 'tensor'), may hold values from -8 to 8
- saved_up: bfloat16 [2, 1024, 14336], P('section', 'dp', 'tensor'), may hold values from -6 to 6
- gate_weight: bfloat16 [2, 8192, 14336], P('section', 'dp', 'tensor'), may hold values from -0.0625 to 0.0625
- up_weight: bfloat16 [2, 8192, 14336], P('section', 'dp', 'tensor'), may hold values from -0.0625 to 0.0625
- down_weight: bfloat16 [2, 14336, 8192], P('section', 'tensor', 'dp'), may hold values from -0.046875 to 0.046875
Outputs:
- fwd_out: bfloat16 [2, 1024, 8192], P('section', 'tensor', 'dp')
- bwd_out: bfloat16 [2, 1024, 8192], P('section', 'tensor', 'dp')
- handed: bfloat16 [2, 1024, 8192], P('section', 'tensor', 'dp')
All inputs are finite; a program needn't handle non-finite values.
Results may differ from a plain program's by a relative error of at most 0.022.
Values may be sent and summed in bfloat16 or wider, within the bound.
No kernel may reach another device: no remote copies, remote signals or barrier semaphores. Data moves between devices by JAX's collectives and lax.ppermute only.
A program may use at most 128 MiB of HBM per device.

v0:
```python
import jax
import jax.numpy as jnp
from jax import lax
from jax.sharding import PartitionSpec as P


def partner(shard, axis, apart):
    return lax.ppermute(shard, axis, [(i, i ^ 1 << apart) for i in range(lax.axis_size(axis))])


def across_rows(part):
    return lax.all_gather(part, "tensor", axis=0, tiled=True)


def feature_total(term):
    return lax.psum_scatter(term, "tensor", scatter_dimension=0, tiled=True)


def transposed(left, right):
    return lax.dot_general(
        left, right, (((1,), (1,)), ((), ())), preferred_element_type=jnp.float32
    )


def local(fwd_in, grad_in, saved_gate, saved_up, gate_weight, up_weight, down_weight):
    inputs = fwd_in[0]
    grads = grad_in[0]
    w_gate = gate_weight[0]
    w_up = up_weight[0]
    w_down = down_weight[0]
    hidden_cols = w_gate.shape[1]
    all_inputs = across_rows(inputs)
    both = jnp.concatenate(
        [
            jnp.dot(all_inputs, w_gate, preferred_element_type=jnp.float32),
            jnp.dot(all_inputs, w_up, preferred_element_type=jnp.float32),
        ],
        axis=1,
    )
    total = lax.psum(both.astype(jnp.bfloat16), "dp").astype(jnp.float32)
    hidden = (jax.nn.silu(total[:, :hidden_cols]) * total[:, hidden_cols:]).astype(jnp.bfloat16)
    mixed_term = jnp.dot(hidden, w_down, preferred_element_type=jnp.float32)
    mixed = feature_total(mixed_term)
    forward_result = (inputs.astype(jnp.float32) + mixed).astype(jnp.bfloat16)
    all_grads = across_rows(grads)
    slope = lax.psum_scatter(
        transposed(all_grads, w_down).astype(jnp.bfloat16), "dp", scatter_dimension=0, tiled=True
    ).astype(jnp.float32)
    gvals = saved_gate[0].astype(jnp.float32)
    uvals = saved_up[0].astype(jnp.float32)
    sig = jax.nn.sigmoid(gvals)
    gate_grad = (slope * uvals * sig * (1.0 + gvals * (1.0 - sig))).astype(jnp.bfloat16)
    up_grad = (slope * gvals * sig).astype(jnp.bfloat16)
    pieces = lax.all_gather((gate_grad, up_grad), "dp", axis=0, tiled=True)
    back_term = transposed(pieces[0], w_gate) + transposed(pieces[1], w_up)
    back = feature_total(back_term)
    backward_result = (grads.astype(jnp.float32) + back).astype(jnp.bfloat16)
    position = lax.axis_index("section")
    outgoing = jnp.where(position == 0, forward_result, backward_result)
    received = partner(outgoing, "section", 0)
    return (forward_result[None], backward_result[None], received[None])


def solution(mesh):
    placed = (
        P("section", "tensor", "dp"),
        P("section", "tensor", "dp"),
        P("section", "dp", "tensor"),
        P("section", "dp", "tensor"),
        P("section", "dp", "tensor"),
        P("section", "dp", "tensor"),
        P("section", "tensor", "dp"),
    )
    return jax.shard_map(
        local,
        mesh=mesh,
        in_specs=placed,
        out_specs=(
            P("section", "tensor", "dp"),
            P("section", "tensor", "dp"),
            P("section", "tensor", "dp"),
        ),
        check_vma=False,
    )
```

profile of v0, /device:TPU:8, one launch (start us, length us, event | category | flops | bytes accessed | tf_op | source)
XLA Modules:
  0.0 895.1 jit_solution(7980363948949293183)
XLA Ops:
  7.2 0.7 all-gather.13.cloned.1.call-update
  8.0 0.7 all-gather.11.cloned.1.call-update
  8.7 0.0 reduce-scatter.6.cloned.1.call-start
  8.7 30.0 %all-gather.13.cloned.1.call-done = bf16[1,1024,512]{2,1,0:T(8,128)(2,1)} async-done(((bf16[1,128,512]{2,1,0:T(8,128)(2,1)}), bf16[1,1024,512]{2,1,0:T(8,128)(2,1)}) %all-gather.13.cloned.1.call-update) | async-done | bytes 1048592 | tf_op jit(solution)/shard_map/all_gather | solution.py:12
  38.7 5.2 convolution_convert_fusion
  43.9 0.0 all-reduce.2.cloned.1.call-start
  44.0 22.4 %all-gather.11.cloned.1.call-done = bf16[1,1024,512]{2,1,0:T(8,128)(2,1)} async-done(((bf16[1,128,512]{2,1,0:T(8,128)(2,1)}), bf16[1,1024,512]{2,1,0:T(8,128)(2,1)}) %all-gather.11.cloned.1.call-update) | async-done | bytes 1048592 | tf_op jit(solution)/shard_map/all_gather | solution.py:12
  66.4 5.9 convolution_convert_fusion.1
  72.3 3.9 convolution_convert_fusion.2
  76.2 6.6 pad_maximum_fusion
  82.8 0.0 all-gather.9.cloned.1.call-start
  82.9 198.7 %reduce-scatter.6.cloned.1.call-done = bf16[64,1792]{1,0:T(8,128)(2,1)} async-done(((bf16[1024,1792]{1,0:T(8,128)(2,1)}), bf16[64,1792]{1,0:T(8,128)(2,1)}) %reduce-scatter.6.cloned.1.call-update) | async-done | bytes 229392 | tf_op jit(solution)/shard_map/reduce_scatter | solution.py:46
  281.6 2.0 fusion.19
  283.7 0.0 all-gather.7.cloned.1.call-start
  283.7 0.5 all-gather.7.cloned.1.call-update
  284.2 0.0 reduce-scatter.4.cloned.1.call-start
  284.3 325.9 %all-reduce.2.cloned.1.call-done = bf16[1024,3584]{1,0:T(8,128)(2,1)} async-done(((bf16[1024,3584]{1,0:T(8,128)(2,1)}), bf16[1024,3584]{1,0:T(8,128)(2,1)}) %all-reduce.2.cloned.1.call-update) | async-done | bytes 7340048 | tf_op jit(solution)/shard_map/psum | solution.py:40
  610.2 10.3 %convert_element_type.44 = f32[1024,3584]{1,0:T(8,128)} convert(bf16[1024,3584]{1,0:T(8,128)(2,1)} %all-reduce.2.cloned.1.call-done) | non-fusion elementwise | flops 3670016 | bytes 22020096 | tf_op jit(solution)/shard_map/convert_element_type | solution.py:40
  620.5 8.6 fusion.1
  629.1 0.0 reduce-scatter.8.cloned.1.call-start
  629.2 82.3 %all-gather.9.cloned.1.call-done = bf16[1024,1792]{1,0:T(8,128)(2,1)} async-done(((bf16[64,1792]{1,0:T(8,128)(2,1)}), bf16[1024,1792]{1,0:T(8,128)(2,1)}) %all-gather.9.cloned.1.call-update) | async-done | bytes 3670032 | tf_op jit(solution)/shard_map/all_gather | solution.py:54
  711.5 6.0 fusion.5
  717.5 89.9 %all-gather.7.cloned.1.call-done = bf16[1024,1792]{1,0:T(8,128)(2,1)} async-done(((bf16[64,1792]{1,0:T(8,128)(2,1)}), bf16[1024,1792]{1,0:T(8,128)(2,1)}) %all-gather.7.cloned.1.call-update) | async-done | bytes 3670032 | tf_op jit(solution)/shard_map/all_gather | solution.py:54
  807.4 6.7 fusion.11
  814.1 29.6 %reduce-scatter.4.cloned.1.call-done = f32[128,512]{1,0:T(8,128)} async-done(((f32[1024,512]{1,0:T(8,128)}), f32[128,512]{1,0:T(8,128)}) %reduce-scatter.4.cloned.1.call-update) | async-done | bytes 262160 | tf_op jit(solution)/shard_map/reduce_scatter | solution.py:16
  843.7 1.6 fusion.29
  845.3 36.1 %reduce-scatter.8.cloned.1.call-done = f32[128,512]{1,0:T(8,128)} async-done(((f32[1024,512]{1,0:T(8,128)}), f32[128,512]{1,0:T(8,128)}) %reduce-scatter.8.cloned.1.call-update) | async-done | bytes 262160 | tf_op jit(solution)/shard_map/reduce_scatter | solution.py:16
  881.5 1.1 broadcast_select_fusion
  882.6 0.7 collective-permute-start
  883.2 1.6 fusion.30
  884.8 2.8 collective-permute-done
  887.6 0.7 copy.12
  (21 shorter events, 0.2 us)
Async XLA Ops:
  7.2 31.5 %copy-start = (bf16[1,1792,512]{2,1,0:T(8,128)(2,1)S(1)}, bf16[1,1792,512]{2,1,0:T(8,128)(2,1)}, u32[]{:S(2)}) copy-start(bf16[1,1792,512]{2,1,0:T(8,128)(2,1)} %param.13) | copy-start | bytes 5505028
  7.2 31.5 %all-gather.13.cloned.1.call-start = ((), (), s32[]{:S(2)}) async-start(), calls=%async_computation.10 | async-start | bytes 1179648 | tf_op jit(solution)/shard_map/all_gather | solution.py:12
  7.9 58.4 %all-gather.11.cloned.1.call-start = ((), (), s32[]{:S(2)}) async-start(), calls=%async_computation.9 | async-start | bytes 1179648 | tf_op jit(solution)/shard_map/all_gather | solution.py:12
  8.7 273.0 %reduce-scatter.6.cloned.1.call-start = ((), (), s32[]{:S(2)}) async-start(), calls=%async_computation.5 | async-start | bytes 3899392 | tf_op jit(solution)/shard_map/reduce_scatter | solution.py:46
  43.9 566.3 %all-reduce.2.cloned.1.call-start = ((), (), s32[]{:S(2)}) async-start(), calls=%async_computation.3 | async-start | bytes 14680064 | tf_op jit(solution)/shard_map/psum | solution.py:40
  66.4 5.9 copy-start.5
  66.4 6.0 copy-start.6
  82.8 198.8 %copy-start.3 = (bf16[1,64,1792]{2,1,0:T(8,128)(2,1)S(1)}, bf16[1,64,1792]{2,1,0:T(8,128)(2,1)}, u32[]{:S(2)}) copy-start(bf16[1,64,1792]{2,1,0:T(8,128)(2,1)} %param.10) | copy-start | bytes 688132
  82.8 198.8 %copy-start.4 = (bf16[1,64,1792]{2,1,0:T(8,128)(2,1)S(1)}, bf16[1,64,1792]{2,1,0:T(8,128)(2,1)}, u32[]{:S(2)}) copy-start(bf16[1,64,1792]{2,1,0:T(8,128)(2,1)} %param.9) | copy-start | bytes 688132
  82.8 628.6 %all-gather.9.cloned.1.call-start = ((), (), s32[]{:S(2)}) async-start(), calls=%async_computation.7 | async-start | bytes 3899392 | tf_op jit(solution)/shard_map/all_gather | solution.py:54
  283.7 523.7 %all-gather.7.cloned.1.call-start = ((), (), s32[]{:S(2)}) async-start(), calls=%async_computation.6 | async-start | bytes 3899392 | tf_op jit(solution)/shard_map/all_gather | solution.py:54
  284.2 559.5 %reduce-scatter.4.cloned.1.call-start = ((), (), s32[]{:S(2)}) async-start(), calls=%async_computation.4 | async-start | bytes 2359296 | tf_op jit(solution)/shard_map/reduce_scatter | solution.py:16
  629.1 252.3 %reduce-scatter.8.cloned.1.call-start = ((), (), s32[]{:S(2)}) async-start(), calls=%async_computation.8 | async-start | bytes 2359296 | tf_op jit(solution)/shard_map/reduce_scatter | solution.py:16
  717.5 126.2 %copy-start.1 = (bf16[1,128,512]{2,1,0:T(8,128)(2,1)S(1)}, bf16[1,128,512]{2,1,0:T(8,128)(2,1)}, u32[]{:S(2)}) copy-start(bf16[1,128,512]{2,1,0:T(8,128)(2,1)} %param.7) | copy-start | bytes 393220
  717.5 163.9 %copy-start.2 = (bf16[1,128,512]{2,1,0:T(8,128)(2,1)S(1)}, bf16[1,128,512]{2,1,0:T(8,128)(2,1)}, u32[]{:S(2)}) copy-start(bf16[1,128,512]{2,1,0:T(8,128)(2,1)} %param.8) | copy-start | bytes 393220
  882.6 5.1 collective-permute-start
Sparse Core Ops, SparseCore 0:
  9.9 28.7 all-gather.12
  40.5 25.7 all-gather.10
  70.4 211.2 reduce-scatter.5
  284.4 325.7 all-reduce.1
  613.0 98.4 all-gather.8
  714.3 93.0 all-gather.6
  810.1 33.5 reduce-scatter.3
  846.4 34.9 reduce-scatter.7
where the time goes:
time: 895 us
  waiting for transfers between devices  820 us (92%)
  matrix products  36.3 us (4%)
  other arithmetic  23.3 us (3%)
  between operations  14.2 us (2%)
    psum x1, waiting for transfers between devices, local(): total = lax.psum(both.astype(jnp.bfloat16), 'dp').astype(jnp.float32)  326 us
    reduce_scatter x1, waiting for transfers between devices, local(): lax.psum_scatter(transposed(all_grads, w_down).astype(jnp.bfloat16), 'dp'...  199 us
    all_gather x2, waiting for transfers between devices, local(): pieces = lax.all_gather((gate_grad, up_grad), 'dp', axis=0, tiled=True)  172 us
    reduce_scatter x2, waiting for transfers between devices, feature_total(): return lax.psum_scatter(term, 'tensor', scatter_dimension=0, tiled=True)  65.7 us
    all_gather x2, waiting for transfers between devices, across_rows(): return lax.all_gather(part, 'tensor', axis=0, tiled=True)  52.3 us
    dot_general x3, matrix products, transposed(): lax.dot_general(left, right, (((1,), (1,)), ((), ())), preferred_element_...  17.9 us
  transfers between devices with their start and end apart: 9, of which 9 were waited for; matrix products, arithmetic and copies ran while one was open for 7% of the time, Pallas kernels for 0%

commit v1 on v0

--- a/solution.py
+++ b/solution.py
@@ -2,6 +2,24 @@
 import jax.numpy as jnp
 from jax import lax
 from jax.sharding import PartitionSpec as P
+
+
+def gather_around(shard, axis, dim):
+    ways, here, step = (lax.axis_size(axis), lax.axis_index(axis), shard.shape[dim])
+    lengths = [n * ways if d == dim else n for d, n in enumerate(shard.shape)]
+    full = lax.dynamic_update_slice_in_dim(
+        jnp.zeros(lengths, shard.dtype), shard, here * step, axis=dim
+    )
+    going_up = going_down = shard
+    for far in range(1, ways // 2 + 1):
+        going_up = lax.ppermute(going_up, axis, [(d, (d + 1) % ways) for d in range(ways)])
+        full = lax.dynamic_update_slice_in_dim(full, going_up, (here - far) % ways * step, axis=dim)
+        if 2 * far < ways:
+            going_down = lax.ppermute(going_down, axis, [(d, (d - 1) % ways) for d in range(ways)])
+            full = lax.dynamic_update_slice_in_dim(
+                full, going_down, (here + far) % ways * step, axis=dim
+            )
+    return full
 
 
 def partner(shard, axis, apart):
@@ -9,7 +27,7 @@
 
 
 def across_rows(part):
-    return lax.all_gather(part, "tensor", axis=0, tiled=True)
+    return gather_around(part, "tensor", 0)
 
 
 def feature_total(term):

time: 895 us -> 860 us (0.961)
  waiting for transfers between devices: 820 us -> 765 us
  starting transfers between devices: 0.98 us -> 18.8 us
    all_gather x2 -> x0, waiting for transfers between devices: 52.3 us -> none  [across_rows(): return lax.all_gather(part, 'tensor', axis=0, tiled=True)]
    reduce_scatter x1, waiting for transfers between devices: 199 us -> 172 us  [local(): lax.psum_scatter(transposed(all_grads, w_down).astype(jnp.bfloat16), 'dp'...]
    ppermute x0 -> x14, waiting for transfers between devices: none -> 25.9 us  [the longest x8 25.9 us: gather_around(): lax.ppermute(going_up, axis, [(d, (d + 1) % ways) for d in range(ways)])]
    ppermute x0 -> x14, starting transfers between devices: none -> 17.8 us  [the longest x6 17.7 us: gather_around(): lax.ppermute(going_down, axis, [(d, (d - 1) % ways) for d in range(ways)])]
  transfers between devices with their start and end apart: 9 -> 21, of which waited for: 9 -> 15; matrix products, arithmetic and copies ran while one was open for 7% -> 6% of each run, Pallas kernels for 0% -> 0%
where the time goes in v1:
time: 860 us; the launch traced here: 859 us
  waiting for transfers between devices  765 us (89%)
  matrix products  34.8 us (4%)
  other arithmetic  23.3 us (3%)
  starting transfers between devices  18.8 us (2%)
  between operations  14.3 us (2%)
    psum x1, waiting for transfers between devices, local(): total = lax.psum(both.astype(jnp.bfloat16), 'dp').astype(jnp.float32)  326 us
    all_gather x2, waiting for transfers between devices, local(): pieces = lax.all_gather((gate_grad, up_grad), 'dp', axis=0, tiled=True)  172 us
    reduce_scatter x1, waiting for transfers between devices, local(): lax.psum_scatter(transposed(all_grads, w_down).astype(jnp.bfloat16), 'dp'...  172 us
    reduce_scatter x2, waiting for transfers between devices, feature_total(): return lax.psum_scatter(term, 'tensor', scatter_dimension=0, tiled=True)  65.5 us
    ppermute x8, waiting for transfers between devices, gather_around(): lax.ppermute(going_up, axis, [(d, (d + 1) % ways) for d in range(ways)])  25.9 us
    ppermute x6, starting transfers between devices, gather_around(): lax.ppermute(going_down, axis, [(d, (d - 1) % ways) for d in range(ways)])  17.7 us
  transfers between devices with their start and end apart: 21, of which 15 were waited for; matrix products, arithmetic and copies ran while one was open for 6% of the time, Pallas kernels for 0%

profile of v1, /device:TPU:8, one launch (start us, length us, event | category | flops | bytes accessed | tf_op | source)
XLA Modules:
  0.0 859.3 jit_solution(4341206345804964824)
XLA Ops:
  7.3 2.9 collective-permute-start.8
  11.2 1.9 collective-permute-done.7
  13.1 3.0 collective-permute-start.10
  16.1 2.6 collective-permute-done.9
  18.7 3.0 collective-permute-start.12
  21.7 2.6 collective-permute-done.11
  24.3 5.5 collective-permute-done.13
  29.9 4.0 convolution_convert_fusion
  34.8 3.0 collective-permute-start.1
  37.9 2.5 collective-permute-done
  40.5 3.0 collective-permute-start.3
  43.4 2.6 collective-permute-done.2
  46.1 3.0 collective-permute-start.5
  49.0 2.6 collective-permute-done.4
  51.7 5.5 collective-permute-done.6
  57.3 5.6 convolution_convert_fusion.1
  62.9 3.9 convolution_convert_fusion.2
  66.8 6.7 pad_maximum_fusion
  73.5 172.1 %reduce-scatter.6.cloned.1.call-done = bf16[64,1792]{1,0:T(8,128)(2,1)} async-done(((bf16[1024,1792]{1,0:T(8,128)(2,1)}), bf16[64,1792]{1,0:T(8,128)(2,1)}) %reduce-scatter.6.cloned.1.call-update) | async-done | bytes 229392 | tf_op jit(solution)/shard_map/reduce_scatter | solution.py:64
  245.6 2.0 fusion.16
  248.2 326.3 %all-reduce.2.cloned.1.call-done = bf16[1024,3584]{1,0:T(8,128)(2,1)} async-done(((bf16[1024,3584]{1,0:T(8,128)(2,1)}), bf16[1024,3584]{1,0:T(8,128)(2,1)}) %all-reduce.2.cloned.1.call-update) | async-done | bytes 7340048 | tf_op jit(solution)/shard_map/psum | solution.py:58
  574.5 10.3 %convert_element_type.44 = f32[1024,3584]{1,0:T(8,128)} convert(bf16[1024,3584]{1,0:T(8,128)(2,1)} %all-reduce.2.cloned.1.call-done) | non-fusion elementwise | flops 3670016 | bytes 22020096 | tf_op jit(solution)/shard_map/convert_element_type | solution.py:58
  584.8 8.6 fusion.1
  593.6 82.3 %all-gather.5.cloned.1.call-done = bf16[1024,1792]{1,0:T(8,128)(2,1)} async-done(((bf16[64,1792]{1,0:T(8,128)(2,1)}), bf16[1024,1792]{1,0:T(8,128)(2,1)}) %all-gather.5.cloned.1.call-update) | async-done | bytes 3670032 | tf_op jit(solution)/shard_map/all_gather | solution.py:72
  676.0 6.0 fusion.5
  682.0 89.9 %all-gather.3.cloned.1.call-done = bf16[1024,1792]{1,0:T(8,128)(2,1)} async-done(((bf16[64,1792]{1,0:T(8,128)(2,1)}), bf16[1024,1792]{1,0:T(8,128)(2,1)}) %all-gather.3.cloned.1.call-update) | async-done | bytes 3670032 | tf_op jit(solution)/shard_map/all_gather | solution.py:72
  771.9 6.7 fusion.11
  778.6 29.5 %reduce-scatter.4.cloned.1.call-done = f32[128,512]{1,0:T(8,128)} async-done(((f32[1024,512]{1,0:T(8,128)}), f32[128,512]{1,0:T(8,128)}) %reduce-scatter.4.cloned.1.call-update) | async-done | bytes 262160 | tf_op jit(solution)/shard_map/reduce_scatter | solution.py:34
  808.0 1.6 fusion.24
  809.6 36.0 %reduce-scatter.8.cloned.1.call-done = f32[128,512]{1,0:T(8,128)} async-done(((f32[1024,512]{1,0:T(8,128)}), f32[128,512]{1,0:T(8,128)}) %reduce-scatter.8.cloned.1.call-update) | async-done | bytes 262160 | tf_op jit(solution)/shard_map/reduce_scatter | solution.py:34
  847.4 1.6 fusion.25
  849.0 2.8 collective-permute-done.14
  (59 shorter events, 5.5 us)
Async XLA Ops:
  7.2 22.7 %copy-start = (bf16[1,1792,512]{2,1,0:T(8,128)(2,1)S(1)}, bf16[1,1792,512]{2,1,0:T(8,128)(2,1)}, u32[]{:S(2)}) copy-start(bf16[1,1792,512]{2,1,0:T(8,128)(2,1)} %param.13) | copy-start | bytes 5505028
  7.2 238.4 %reduce-scatter.6.cloned.1.call-start = ((), (), s32[]{:S(2)}) async-start(), calls=%async_computation.5 | async-start | bytes 3899392 | tf_op jit(solution)/shard_map/reduce_scatter | solution.py:64
  7.2 5.8 collective-permute-start.7
  7.3 5.8 collective-permute-start.8
  13.1 5.6 collective-permute-start.9
  13.1 5.6 collective-permute-start.10
  18.7 5.6 collective-permute-start.11
  18.7 5.6 collective-permute-start.12
  24.3 5.6 collective-permute-start.13
  33.9 0.9 copy-start.1
  33.9 540.6 %all-reduce.2.cloned.1.call-start = ((), (), s32[]{:S(2)}) async-start(), calls=%async_computation.3 | async-start | bytes 14680064 | tf_op jit(solution)/shard_map/psum | solution.py:58
  34.8 5.6 collective-permute-start
  34.8 5.6 collective-permute-start.1
  40.4 5.6 collective-permute-start.2
  40.5 5.6 collective-permute-start.3
  46.0 5.6 collective-permute-start.4
  46.1 5.6 collective-permute-start.5
  51.6 5.6 collective-permute-start.6
  57.3 5.6 copy-start.5
  73.4 172.2 %copy-start.3 = (bf16[1,64,1792]{2,1,0:T(8,128)(2,1)S(1)}, bf16[1,64,1792]{2,1,0:T(8,128)(2,1)}, u32[]{:S(2)}) copy-start(bf16[1,64,1792]{2,1,0:T(8,128)(2,1)} %param.10) | copy-start | bytes 688132
  73.4 172.2 %copy-start.4 = (bf16[1,64,1792]{2,1,0:T(8,128)(2,1)S(1)}, bf16[1,64,1792]{2,1,0:T(8,128)(2,1)}, u32[]{:S(2)}) copy-start(bf16[1,64,1792]{2,1,0:T(8,128)(2,1)} %param.9) | copy-start | bytes 688132
  73.4 602.5 %all-gather.5.cloned.1.call-start = ((), (), s32[]{:S(2)}) async-start(), calls=%async_computation.7 | async-start | bytes 3899392 | tf_op jit(solution)/shard_map/all_gather | solution.py:72
  247.6 524.2 %all-gather.3.cloned.1.call-start = ((), (), s32[]{:S(2)}) async-start(), calls=%async_computation.6 | async-start | bytes 3899392 | tf_op jit(solution)/shard_map/all_gather | solution.py:72
  248.2 559.8 %reduce-scatter.4.cloned.1.call-start = ((), (), s32[]{:S(2)}) async-start(), calls=%async_computation.4 | async-start | bytes 2359296 | tf_op jit(solution)/shard_map/reduce_scatter | solution.py:34
  593.4 252.3 %reduce-scatter.8.cloned.1.call-start = ((), (), s32[]{:S(2)}) async-start(), calls=%async_computation.8 | async-start | bytes 2359296 | tf_op jit(solution)/shard_map/reduce_scatter | solution.py:34
  682.0 163.7 %copy-start.2 = (bf16[1,128,512]{2,1,0:T(8,128)(2,1)S(1)}, bf16[1,128,512]{2,1,0:T(8,128)(2,1)}, u32[]{:S(2)}) copy-start(bf16[1,128,512]{2,1,0:T(8,128)(2,1)} %param.8) | copy-start | bytes 393220
  846.8 5.1 collective-permute-start.14
Sparse Core Ops, SparseCore 0:
  34.1 211.4 reduce-scatter.5
  248.5 325.9 all-reduce.1
  577.4 98.4 all-gather.4
  678.7 93.0 all-gather.2
  774.4 33.5 reduce-scatter.3
  810.6 35.0 reduce-scatter.7
